TPU v7x, 256 devices: a whole 4x4x8 slice. The times are simulated.
256 devices in a mesh: shot: 4 (over x_hi, core), space: 64 (over x_lo, y, z).
Axes of the slice: x: 4 (x_hi: 2, x_lo: 2; x = x_hi * 2 + x_lo), y: 4, z: 8, core: 2. Of those that a mesh axis runs over, the one named last changes fastest.
Arguments:
- residual_traces: float32 [4, 12, 16384], P('shot', None, 'space'), may hold values from -6 to 6
- owners: int32 [4, 16384, 1], P('shot', 'space'), may hold values from 0 to 63; in each aligned block of 256 rows (0 to 255, 256 to 511, ..., all dimensions but the last counted through in order) at most 8 rows name the same one
- surface_cells: int32 [4, 16384], P('shot', 'space'), may hold values from 0 to 511
- trace_counts: int32 [4], P('shot'), may hold values from 4096 to 16384, as said below
- start_current: float32 [4, 512, 64, 256], P('shot', 'space'), may hold values from -6 to 6
- start_later: float32 [4, 512, 64, 256], P('shot', 'space'), may hold values from -6 to 6
- forward_accel: bfloat16 [4, 12, 512, 64, 256], P('shot', None, 'space'), may hold values from -6 to 6
- courant_sq: float32 [512, 64, 256], P('space'), may hold values from 0.04 to 0.16
Outputs:
- adjoint_field: float32 [4, 512, 64, 256], P('shot', 'space')
- velocity_grad: float32 [512, 64, 256], P('space', 'shot')
Inputs may be any that keep to these rules, and one draw needn't show every extreme that they name: `owners`: among the receivers of one device, no subdomain is named more than 8 times. `trace_counts`: some shot has all 16384 traces live.
All inputs are finite; a program needn't handle non-finite values.
Results may differ from a plain program's by a relative error of at most 0.0003.
Values sent between devices are 32-bit elements; how exact they have to be, the bound alone decides.
A program may use at most 64 MiB of HBM per device.

v0:
```python
import jax
import jax.numpy as jnp
from jax import lax
from jax.sharding import PartitionSpec as P

STENCIL_WEIGHTS = (-205.0 / 72.0, 8.0 / 5.0, -1.0 / 5.0, 8.0 / 315.0, -1.0 / 560.0)


def extended_2(shard, sides, width):
    for axis, dim in sides:
        size, length = (lax.axis_size(axis), shard.shape[dim])
        up = [(i, (i + 1) % size) for i in range(size - 1)]
        down = [(j, i) for i, j in up]
        last = lax.slice_in_dim(shard, length - width, length, axis=dim)
        leading = lax.slice_in_dim(shard, 0, width, axis=dim)
        before = lax.ppermute(last, axis, up)
        after = lax.ppermute(leading, axis, down)
        shard = jnp.concatenate([before, shard, after], axis=dim)
    return shard


def laplace(padded):
    length = padded.shape[0] - 8
    across = padded.shape[1] - 8
    height = padded.shape[2] - 8

    def window(off_x, off_y, off_z):
        return lax.slice(
            padded,
            (4 + off_x, 4 + off_y, 4 + off_z),
            (4 + off_x + length, 4 + off_y + across, 4 + off_z + height),
        )

    summed = 3.0 * STENCIL_WEIGHTS[0] * window(0, 0, 0)
    for offset in range(1, 5):
        six_taps = window(offset, 0, 0) + window(-offset, 0, 0) + window(0, offset, 0)
        six_taps = six_taps + window(0, -offset, 0) + window(0, 0, offset) + window(0, 0, -offset)
        summed = summed + STENCIL_WEIGHTS[offset] * six_taps
    return summed


def laplace_rim(extended):
    return laplace(jnp.pad(extended, ((0, 0), (4, 4), (4, 4))))


def onehot_cells(targets, plane_cells):
    return (targets[:, None] == jnp.arange(plane_cells, dtype=jnp.int32)[None, :]).astype(
        jnp.float32
    )


def shards(
    residual_traces,
    owners,
    surface_cells,
    trace_counts,
    start_current,
    start_later,
    forward_accel,
    courant_sq,
):
    traces = residual_traces[0]
    owner_row = owners[0, :, 0]
    surface = surface_cells[0]
    live_count = trace_counts[0]
    forward = forward_accel[0]
    first_field = start_current[0]
    prior_field = start_later[0]
    length, across, height = courant_sq.shape
    plane_cells = length * across
    steps_all = traces.shape[0]
    my_index = lax.axis_index("space")
    piece_traces = lax.all_gather(traces, "space", axis=1, tiled=True)
    piece_owner = lax.all_gather(owner_row[None, :], "space", axis=1, tiled=True)
    piece_surface = lax.all_gather(surface[None, :], "space", axis=1, tiled=True)
    number = jnp.arange(piece_traces.shape[1], dtype=jnp.int32)
    keep = (number < live_count) & (piece_owner[0] == my_index)
    targets = jnp.where(keep, piece_surface[0], -1)
    table = onehot_cells(targets, plane_cells)
    planes = jnp.dot(
        piece_traces, table, precision=lax.Precision.HIGHEST, preferred_element_type=jnp.float32
    )
    planes = planes.reshape(steps_all, length, across)
    empty = jnp.zeros((length, across, height), jnp.float32)

    def advance(section, state):
        current, later, gradient = state
        extended = extended_2(current, (("space", 0),), 4)
        fresh = 2.0 * current - later + courant_sq * laplace_rim(extended)
        fresh = fresh.at[:, :, 2].add(lax.dynamic_index_in_dim(planes, section, 0, keepdims=False))
        accel = lax.dynamic_index_in_dim(forward, section, 0, keepdims=False).astype(jnp.float32)
        return (fresh, current, gradient + fresh * accel)

    current, later, gradient = lax.fori_loop(
        0, steps_all, advance, (first_field, prior_field, empty)
    )
    velocity_grad = lax.psum_scatter(gradient, "shot", scatter_dimension=1, tiled=True)
    return (current[None], velocity_grad)


def solution(mesh):
    placed = (
        P("shot", None, "space"),
        P("shot", "space", None),
        P("shot", "space"),
        P("shot"),
        P("shot", "space", None, None),
        P("shot", "space", None, None),
        P("shot", None, "space", None, None),
        P("space", None, None),
    )
    return jax.shard_map(
        shards,
        mesh=mesh,
        in_specs=placed,
        out_specs=(P("shot", "space", None, None), P("space", "shot", None)),
        check_vma=False,
    )
```

profile of v0, /device:TPU:2, one launch (start us, length us, event | category | flops | bytes accessed | tf_op | source)
XLA Modules:
  0.0 967.2 jit_solution(18248099924798978966)
XLA Ops:
  7.9 158.5 %all-gather = s32[1,16384,1]{1,2,0:T(1,128)S(1)} all-gather(s32[1,256,1]{1,2,0:T(1,128)} %param.13), channel_id=2, replica_groups=mesh['shot'=4,'space'=64] {'space'}, dimensions={1}, use_global_device_ids=true | all-gather | bytes 66560 | tf_op jit(solution)/shard_map/all_gather | solution.py:74
  166.3 150.3 %all_gather.10 = s32[1,16384]{1,0:T(1,128)S(1)} all-gather(s32[1,256]{1,0:T(1,128)} %param.14), channel_id=1, replica_groups=mesh['shot'=4,'space'=64] {'space'}, dimensions={1}, use_global_device_ids=true | all-gather | bytes 66560 | tf_op jit(solution)/shard_map/all_gather | solution.py:75
  316.6 156.5 %all-gather.1 = f32[1,12,16384]{2,0,1:T(1,128)S(1)} all-gather(f32[1,12,256]{2,0,1:T(1,128)} %param.12), channel_id=3, replica_groups=mesh['shot'=4,'space'=64] {'space'}, dimensions={2}, use_global_device_ids=true | all-gather | bytes 798720 | tf_op jit(solution)/shard_map/all_gather | solution.py:73
  473.4 10.6 %fusion.36 = f32[12,512]{1,0:T(8,128)S(1)} fusion(s32[16384]{0:T(1024)S(1)} %fusion.40, f32[1,12,16384]{2,0,1:T(1,128)S(1)} %all-gather.1), kind=kOutput, calls=%fused_computation.58 | convolution fusion | flops 1216348160 | bytes 876544 | tf_op jit(solution)/shard_map/dot_general | solution.py:80
  487.2 7.0 copy.36
  494.3 437.1 %while.21 = (s32[]{:T(128)}, f32[8,64,256]{1,0,2:T(8,128)S(1)}, f32[8,64,256]{1,0,2:T(8,128)}, f32[8,64,256]{1,0,2:T(8,128)}, f32[8,64,256]{1,0,2:T(8,128)}, /*i...) while((s32[]{:T(128)}, f32[8,64,256]{1,0,2:T(8,128)S(1)}, ...), condition=%wide.region_1.2_spmd.clone, body=%wide.region_0.1_spmd.clone.sunk | while | flops 9936387 | bytes 35305808 | solution.py:94
  514.2 10.2 %fusion.47 = f32[8,64,256]{1,0,2:T(8,128)} fusion(f32[8,64,256]{1,0,2:T(8,128)} %get-tuple-element.335, f32[8,64,256]{1,0,2:T(8,128)S(1)} %get-tuple-element.323, f32[4,64,256]{1,0,2:T(4,128)} %collective-permute-done, f32[16,72,264]{1,0,2:T(8,128)S(1)} %select_maximum_fusion.3, f32[12,64,256]{1,0,2:T(8,128)} %copy-done, ...), kind=kLoop, calls=%fused_computation.25.clone.1 | loop fusion | flops 4849664 | bytes 12845056 | tf_op jit(solution)/shard_map/while/body/eval_jaxpr/add | solution.py:89
  550.6 10.2 %fusion.47 = f32[8,64,256]{1,0,2:T(8,128)} fusion(f32[8,64,256]{1,0,2:T(8,128)} %get-tuple-element.335, f32[8,64,256]{1,0,2:T(8,128)S(1)} %get-tuple-element.323, f32[4,64,256]{1,0,2:T(4,128)} %collective-permute-done, f32[16,72,264]{1,0,2:T(8,128)S(1)} %select_maximum_fusion.3, f32[12,64,256]{1,0,2:T(8,128)} %copy-done, ...), kind=kLoop, calls=%fused_computation.25.clone.1 | loop fusion | flops 4849664 | bytes 12845056 | tf_op jit(solution)/shard_map/while/body/eval_jaxpr/add | solution.py:89
  573.2 5.1 collective-permute-done.1
  587.0 10.2 %fusion.47 = f32[8,64,256]{1,0,2:T(8,128)} fusion(f32[8,64,256]{1,0,2:T(8,128)} %get-tuple-element.335, f32[8,64,256]{1,0,2:T(8,128)S(1)} %get-tuple-element.323, f32[4,64,256]{1,0,2:T(4,128)} %collective-permute-done, f32[16,72,264]{1,0,2:T(8,128)S(1)} %select_maximum_fusion.3, f32[12,64,256]{1,0,2:T(8,128)} %copy-done, ...), kind=kLoop, calls=%fused_computation.25.clone.1 | loop fusion | flops 4849664 | bytes 12845056 | tf_op jit(solution)/shard_map/while/body/eval_jaxpr/add | solution.py:89
  623.5 10.2 %fusion.47 = f32[8,64,256]{1,0,2:T(8,128)} fusion(f32[8,64,256]{1,0,2:T(8,128)} %get-tuple-element.335, f32[8,64,256]{1,0,2:T(8,128)S(1)} %get-tuple-element.323, f32[4,64,256]{1,0,2:T(4,128)} %collective-permute-done, f32[16,72,264]{1,0,2:T(8,128)S(1)} %select_maximum_fusion.3, f32[12,64,256]{1,0,2:T(8,128)} %copy-done, ...), kind=kLoop, calls=%fused_computation.25.clone.1 | loop fusion | flops 4849664 | bytes 12845056 | tf_op jit(solution)/shard_map/while/body/eval_jaxpr/add | solution.py:89
  646.0 5.1 collective-permute-done.1
  659.9 10.2 %fusion.47 = f32[8,64,256]{1,0,2:T(8,128)} fusion(f32[8,64,256]{1,0,2:T(8,128)} %get-tuple-element.335, f32[8,64,256]{1,0,2:T(8,128)S(1)} %get-tuple-element.323, f32[4,64,256]{1,0,2:T(4,128)} %collective-permute-done, f32[16,72,264]{1,0,2:T(8,128)S(1)} %select_maximum_fusion.3, f32[12,64,256]{1,0,2:T(8,128)} %copy-done, ...), kind=kLoop, calls=%fused_computation.25.clone.1 | loop fusion | flops 4849664 | bytes 12845056 | tf_op jit(solution)/shard_map/while/body/eval_jaxpr/add | solution.py:89
  696.3 10.2 %fusion.47 = f32[8,64,256]{1,0,2:T(8,128)} fusion(f32[8,64,256]{1,0,2:T(8,128)} %get-tuple-element.335, f32[8,64,256]{1,0,2:T(8,128)S(1)} %get-tuple-element.323, f32[4,64,256]{1,0,2:T(4,128)} %collective-permute-done, f32[16,72,264]{1,0,2:T(8,128)S(1)} %select_maximum_fusion.3, f32[12,64,256]{1,0,2:T(8,128)} %copy-done, ...), kind=kLoop, calls=%fused_computation.25.clone.1 | loop fusion | flops 4849664 | bytes 12845056 | tf_op jit(solution)/shard_map/while/body/eval_jaxpr/add | solution.py:89
  718.9 5.1 collective-permute-done.1
  732.7 10.2 %fusion.47 = f32[8,64,256]{1,0,2:T(8,128)} fusion(f32[8,64,256]{1,0,2:T(8,128)} %get-tuple-element.335, f32[8,64,256]{1,0,2:T(8,128)S(1)} %get-tuple-element.323, f32[4,64,256]{1,0,2:T(4,128)} %collective-permute-done, f32[16,72,264]{1,0,2:T(8,128)S(1)} %select_maximum_fusion.3, f32[12,64,256]{1,0,2:T(8,128)} %copy-done, ...), kind=kLoop, calls=%fused_computation.25.clone.1 | loop fusion | flops 4849664 | bytes 12845056 | tf_op jit(solution)/shard_map/while/body/eval_jaxpr/add | solution.py:89
  755.3 5.1 collective-permute-done.1
  769.2 10.2 %fusion.47 = f32[8,64,256]{1,0,2:T(8,128)} fusion(f32[8,64,256]{1,0,2:T(8,128)} %get-tuple-element.335, f32[8,64,256]{1,0,2:T(8,128)S(1)} %get-tuple-element.323, f32[4,64,256]{1,0,2:T(4,128)} %collective-permute-done, f32[16,72,264]{1,0,2:T(8,128)S(1)} %select_maximum_fusion.3, f32[12,64,256]{1,0,2:T(8,128)} %copy-done, ...), kind=kLoop, calls=%fused_computation.25.clone.1 | loop fusion | flops 4849664 | bytes 12845056 | tf_op jit(solution)/shard_map/while/body/eval_jaxpr/add | solution.py:89
  805.6 10.2 %fusion.47 = f32[8,64,256]{1,0,2:T(8,128)} fusion(f32[8,64,256]{1,0,2:T(8,128)} %get-tuple-element.335, f32[8,64,256]{1,0,2:T(8,128)S(1)} %get-tuple-element.323, f32[4,64,256]{1,0,2:T(4,128)} %collective-permute-done, f32[16,72,264]{1,0,2:T(8,128)S(1)} %select_maximum_fusion.3, f32[12,64,256]{1,0,2:T(8,128)} %copy-done, ...), kind=kLoop, calls=%fused_computation.25.clone.1 | loop fusion | flops 4849664 | bytes 12845056 | tf_op jit(solution)/shard_map/while/body/eval_jaxpr/add | solution.py:89
  828.2 5.1 collective-permute-done.1
  842.0 10.2 %fusion.47 = f32[8,64,256]{1,0,2:T(8,128)} fusion(f32[8,64,256]{1,0,2:T(8,128)} %get-tuple-element.335, f32[8,64,256]{1,0,2:T(8,128)S(1)} %get-tuple-element.323, f32[4,64,256]{1,0,2:T(4,128)} %collective-permute-done, f32[16,72,264]{1,0,2:T(8,128)S(1)} %select_maximum_fusion.3, f32[12,64,256]{1,0,2:T(8,128)} %copy-done, ...), kind=kLoop, calls=%fused_computation.25.clone.1 | loop fusion | flops 4849664 | bytes 12845056 | tf_op jit(solution)/shard_map/while/body/eval_jaxpr/add | solution.py:89
  878.4 10.2 %fusion.47 = f32[8,64,256]{1,0,2:T(8,128)} fusion(f32[8,64,256]{1,0,2:T(8,128)} %get-tuple-element.335, f32[8,64,256]{1,0,2:T(8,128)S(1)} %get-tuple-element.323, f32[4,64,256]{1,0,2:T(4,128)} %collective-permute-done, f32[16,72,264]{1,0,2:T(8,128)S(1)} %select_maximum_fusion.3, f32[12,64,256]{1,0,2:T(8,128)} %copy-done, ...), kind=kLoop, calls=%fused_computation.25.clone.1 | loop fusion | flops 4849664 | bytes 12845056 | tf_op jit(solution)/shard_map/while/body/eval_jaxpr/add | solution.py:89
  914.9 10.2 %fusion.47 = f32[8,64,256]{1,0,2:T(8,128)} fusion(f32[8,64,256]{1,0,2:T(8,128)} %get-tuple-element.335, f32[8,64,256]{1,0,2:T(8,128)S(1)} %get-tuple-element.323, f32[4,64,256]{1,0,2:T(4,128)} %collective-permute-done, f32[16,72,264]{1,0,2:T(8,128)S(1)} %select_maximum_fusion.3, f32[12,64,256]{1,0,2:T(8,128)} %copy-done, ...), kind=kLoop, calls=%fused_computation.25.clone.1 | loop fusion | flops 4849664 | bytes 12845056 | tf_op jit(solution)/shard_map/while/body/eval_jaxpr/add | solution.py:89
  934.9 25.5 %reduce-scatter.2.cloned.1.call-done = f32[8,16,256]{2,1,0:T(8,128)} async-done(((f32[8,64,256]{2,1,0:T(8,128)}), f32[8,16,256]{2,1,0:T(8,128)}) %reduce-scatter.2.cloned.1.call-update) | async-done | bytes 131088 | tf_op jit(solution)/shard_map/reduce_scatter | solution.py:97
  (276 shorter events, 295.6 us)
Async XLA Ops:
  7.2 953.2 %reduce-scatter.2.cloned.1.call-start = ((), (), s32[]{:S(2)}) async-start(), calls=%async_computation.1 | async-start | bytes 655360 | tf_op jit(solution)/shard_map/reduce_scatter | solution.py:97
  494.4 11.1 %collective-permute-start.1 = (f32[4,64,256]{1,0,2:T(4,128)S(1)}, f32[4,64,256]{1,0,2:T(4,128)S(1)}, u32[]{:S(2)}, u32[]{:S(2)}) collective-permute-start(f32[4,64,256]{1,0,2:T(4,128)S(1)} %get-tuple-element.312), channel_id=1, source_target_pairs={{1,0},{2,1},{3,2},{4,3},{5,4},{6,5},{7,6},{8,7},{9,8},{10,9},{11,1... | collective-permute-start | bytes 786440 | tf_op jit(solution)/shard_map/while/body/eval_jaxpr/ppermute | solution.py:17
  496.4 15.4 %collective-permute-start = (f32[4,64,256]{1,0,2:T(4,128)S(1)}, f32[4,64,256]{1,0,2:T(4,128)}, u32[]{:S(2)}, u32[]{:S(2)}) collective-permute-start(f32[4,64,256]{1,0,2:T(4,128)S(1)} %get-tuple-element.311), channel_id=1, source_target_pairs={{0,1},{1,2},{2,3},{3,4},{4,5},{5,6},{6,7},{7,8},{8,9},{9,10},{10,1... | collective-permute-start | bytes 786440 | tf_op jit(solution)/shard_map/while/body/eval_jaxpr/ppermute | solution.py:16
  530.8 11.1 %collective-permute-start.1 = (f32[4,64,256]{1,0,2:T(4,128)S(1)}, f32[4,64,256]{1,0,2:T(4,128)S(1)}, u32[]{:S(2)}, u32[]{:S(2)}) collective-permute-start(f32[4,64,256]{1,0,2:T(4,128)S(1)} %get-tuple-element.312), channel_id=1, source_target_pairs={{1,0},{2,1},{3,2},{4,3},{5,4},{6,5},{7,6},{8,7},{9,8},{10,9},{11,1... | collective-permute-start | bytes 786440 | tf_op jit(solution)/shard_map/while/body/eval_jaxpr/ppermute | solution.py:17
  532.8 15.4 %collective-permute-start = (f32[4,64,256]{1,0,2:T(4,128)S(1)}, f32[4,64,256]{1,0,2:T(4,128)}, u32[]{:S(2)}, u32[]{:S(2)}) collective-permute-start(f32[4,64,256]{1,0,2:T(4,128)S(1)} %get-tuple-element.311), channel_id=1, source_target_pairs={{0,1},{1,2},{2,3},{3,4},{4,5},{5,6},{6,7},{7,8},{8,9},{9,10},{10,1... | collective-permute-start | bytes 786440 | tf_op jit(solution)/shard_map/while/body/eval_jaxpr/ppermute | solution.py:16
  567.2 11.1 %collective-permute-start.1 = (f32[4,64,256]{1,0,2:T(4,128)S(1)}, f32[4,64,256]{1,0,2:T(4,128)S(1)}, u32[]{:S(2)}, u32[]{:S(2)}) collective-permute-start(f32[4,64,256]{1,0,2:T(4,128)S(1)} %get-tuple-element.312), channel_id=1, source_target_pairs={{1,0},{2,1},{3,2},{4,3},{5,4},{6,5},{7,6},{8,7},{9,8},{10,9},{11,1... | collective-permute-start | bytes 786440 | tf_op jit(solution)/shard_map/while/body/eval_jaxpr/ppermute | solution.py:17
  569.3 15.4 %collective-permute-start = (f32[4,64,256]{1,0,2:T(4,128)S(1)}, f32[4,64,256]{1,0,2:T(4,128)}, u32[]{:S(2)}, u32[]{:S(2)}) collective-permute-start(f32[4,64,256]{1,0,2:T(4,128)S(1)} %get-tuple-element.311), channel_id=1, source_target_pairs={{0,1},{1,2},{2,3},{3,4},{4,5},{5,6},{6,7},{7,8},{8,9},{9,10},{10,1... | collective-permute-start | bytes 786440 | tf_op jit(solution)/shard_map/while/body/eval_jaxpr/ppermute | solution.py:16
  603.7 11.1 %collective-permute-start.1 = (f32[4,64,256]{1,0,2:T(4,128)S(1)}, f32[4,64,256]{1,0,2:T(4,128)S(1)}, u32[]{:S(2)}, u32[]{:S(2)}) collective-permute-start(f32[4,64,256]{1,0,2:T(4,128)S(1)} %get-tuple-element.312), channel_id=1, source_target_pairs={{1,0},{2,1},{3,2},{4,3},{5,4},{6,5},{7,6},{8,7},{9,8},{10,9},{11,1... | collective-permute-start | bytes 786440 | tf_op jit(solution)/shard_map/while/body/eval_jaxpr/ppermute | solution.py:17
  605.7 15.4 %collective-permute-start = (f32[4,64,256]{1,0,2:T(4,128)S(1)}, f32[4,64,256]{1,0,2:T(4,128)}, u32[]{:S(2)}, u32[]{:S(2)}) collective-permute-start(f32[4,64,256]{1,0,2:T(4,128)S(1)} %get-tuple-element.311), channel_id=1, source_target_pairs={{0,1},{1,2},{2,3},{3,4},{4,5},{5,6},{6,7},{7,8},{8,9},{9,10},{10,1... | collective-permute-start | bytes 786440 | tf_op jit(solution)/shard_map/while/body/eval_jaxpr/ppermute | solution.py:16
  640.1 11.1 %collective-permute-start.1 = (f32[4,64,256]{1,0,2:T(4,128)S(1)}, f32[4,64,256]{1,0,2:T(4,128)S(1)}, u32[]{:S(2)}, u32[]{:S(2)}) collective-permute-start(f32[4,64,256]{1,0,2:T(4,128)S(1)} %get-tuple-element.312), channel_id=1, source_target_pairs={{1,0},{2,1},{3,2},{4,3},{5,4},{6,5},{7,6},{8,7},{9,8},{10,9},{11,1... | collective-permute-start | bytes 786440 | tf_op jit(solution)/shard_map/while/body/eval_jaxpr/ppermute | solution.py:17
  642.1 15.4 %collective-permute-start = (f32[4,64,256]{1,0,2:T(4,128)S(1)}, f32[4,64,256]{1,0,2:T(4,128)}, u32[]{:S(2)}, u32[]{:S(2)}) collective-permute-start(f32[4,64,256]{1,0,2:T(4,128)S(1)} %get-tuple-element.311), channel_id=1, source_target_pairs={{0,1},{1,2},{2,3},{3,4},{4,5},{5,6},{6,7},{7,8},{8,9},{9,10},{10,1... | collective-permute-start | bytes 786440 | tf_op jit(solution)/shard_map/while/body/eval_jaxpr/ppermute | solution.py:16
  676.5 11.1 %collective-permute-start.1 = (f32[4,64,256]{1,0,2:T(4,128)S(1)}, f32[4,64,256]{1,0,2:T(4,128)S(1)}, u32[]{:S(2)}, u32[]{:S(2)}) collective-permute-start(f32[4,64,256]{1,0,2:T(4,128)S(1)} %get-tuple-element.312), channel_id=1, source_target_pairs={{1,0},{2,1},{3,2},{4,3},{5,4},{6,5},{7,6},{8,7},{9,8},{10,9},{11,1... | collective-permute-start | bytes 786440 | tf_op jit(solution)/shard_map/while/body/eval_jaxpr/ppermute | solution.py:17
  678.6 15.4 %collective-permute-start = (f32[4,64,256]{1,0,2:T(4,128)S(1)}, f32[4,64,256]{1,0,2:T(4,128)}, u32[]{:S(2)}, u32[]{:S(2)}) collective-permute-start(f32[4,64,256]{1,0,2:T(4,128)S(1)} %get-tuple-element.311), channel_id=1, source_target_pairs={{0,1},{1,2},{2,3},{3,4},{4,5},{5,6},{6,7},{7,8},{8,9},{9,10},{10,1... | collective-permute-start | bytes 786440 | tf_op jit(solution)/shard_map/while/body/eval_jaxpr/ppermute | solution.py:16
  712.9 11.1 %collective-permute-start.1 = (f32[4,64,256]{1,0,2:T(4,128)S(1)}, f32[4,64,256]{1,0,2:T(4,128)S(1)}, u32[]{:S(2)}, u32[]{:S(2)}) collective-permute-start(f32[4,64,256]{1,0,2:T(4,128)S(1)} %get-tuple-element.312), channel_id=1, source_target_pairs={{1,0},{2,1},{3,2},{4,3},{5,4},{6,5},{7,6},{8,7},{9,8},{10,9},{11,1... | collective-permute-start | bytes 786440 | tf_op jit(solution)/shard_map/while/body/eval_jaxpr/ppermute | solution.py:17
  715.0 15.4 %collective-permute-start = (f32[4,64,256]{1,0,2:T(4,128)S(1)}, f32[4,64,256]{1,0,2:T(4,128)}, u32[]{:S(2)}, u32[]{:S(2)}) collective-permute-start(f32[4,64,256]{1,0,2:T(4,128)S(1)} %get-tuple-element.311), channel_id=1, source_target_pairs={{0,1},{1,2},{2,3},{3,4},{4,5},{5,6},{6,7},{7,8},{8,9},{9,10},{10,1... | collective-permute-start | bytes 786440 | tf_op jit(solution)/shard_map/while/body/eval_jaxpr/ppermute | solution.py:16
  749.4 11.1 %collective-permute-start.1 = (f32[4,64,256]{1,0,2:T(4,128)S(1)}, f32[4,64,256]{1,0,2:T(4,128)S(1)}, u32[]{:S(2)}, u32[]{:S(2)}) collective-permute-start(f32[4,64,256]{1,0,2:T(4,128)S(1)} %get-tuple-element.312), channel_id=1, source_target_pairs={{1,0},{2,1},{3,2},{4,3},{5,4},{6,5},{7,6},{8,7},{9,8},{10,9},{11,1... | collective-permute-start | bytes 786440 | tf_op jit(solution)/shard_map/while/body/eval_jaxpr/ppermute | solution.py:17
  751.4 15.4 %collective-permute-start = (f32[4,64,256]{1,0,2:T(4,128)S(1)}, f32[4,64,256]{1,0,2:T(4,128)}, u32[]{:S(2)}, u32[]{:S(2)}) collective-permute-start(f32[4,64,256]{1,0,2:T(4,128)S(1)} %get-tuple-element.311), channel_id=1, source_target_pairs={{0,1},{1,2},{2,3},{3,4},{4,5},{5,6},{6,7},{7,8},{8,9},{9,10},{10,1... | collective-permute-start | bytes 786440 | tf_op jit(solution)/shard_map/while/body/eval_jaxpr/ppermute | solution.py:16
  787.8 15.4 %collective-permute-start = (f32[4,64,256]{1,0,2:T(4,128)S(1)}, f32[4,64,256]{1,0,2:T(4,128)}, u32[]{:S(2)}, u32[]{:S(2)}) collective-permute-start(f32[4,64,256]{1,0,2:T(4,128)S(1)} %get-tuple-element.311), channel_id=1, source_target_pairs={{0,1},{1,2},{2,3},{3,4},{4,5},{5,6},{6,7},{7,8},{8,9},{9,10},{10,1... | collective-permute-start | bytes 786440 | tf_op jit(solution)/shard_map/while/body/eval_jaxpr/ppermute | solution.py:16
  822.2 11.1 %collective-permute-start.1 = (f32[4,64,256]{1,0,2:T(4,128)S(1)}, f32[4,64,256]{1,0,2:T(4,128)S(1)}, u32[]{:S(2)}, u32[]{:S(2)}) collective-permute-start(f32[4,64,256]{1,0,2:T(4,128)S(1)} %get-tuple-element.312), channel_id=1, source_target_pairs={{1,0},{2,1},{3,2},{4,3},{5,4},{6,5},{7,6},{8,7},{9,8},{10,9},{11,1... | collective-permute-start | bytes 786440 | tf_op jit(solution)/shard_map/while/body/eval_jaxpr/ppermute | solution.py:17
  824.3 15.4 %collective-permute-start = (f32[4,64,256]{1,0,2:T(4,128)S(1)}, f32[4,64,256]{1,0,2:T(4,128)}, u32[]{:S(2)}, u32[]{:S(2)}) collective-permute-start(f32[4,64,256]{1,0,2:T(4,128)S(1)} %get-tuple-element.311), channel_id=1, source_target_pairs={{0,1},{1,2},{2,3},{3,4},{4,5},{5,6},{6,7},{7,8},{8,9},{9,10},{10,1... | collective-permute-start | bytes 786440 | tf_op jit(solution)/shard_map/while/body/eval_jaxpr/ppermute | solution.py:16
  858.6 11.1 %collective-permute-start.1 = (f32[4,64,256]{1,0,2:T(4,128)S(1)}, f32[4,64,256]{1,0,2:T(4,128)S(1)}, u32[]{:S(2)}, u32[]{:S(2)}) collective-permute-start(f32[4,64,256]{1,0,2:T(4,128)S(1)} %get-tuple-element.312), channel_id=1, source_target_pairs={{1,0},{2,1},{3,2},{4,3},{5,4},{6,5},{7,6},{8,7},{9,8},{10,9},{11,1... | collective-permute-start | bytes 786440 | tf_op jit(solution)/shard_map/while/body/eval_jaxpr/ppermute | solution.py:17
  860.7 15.4 %collective-permute-start = (f32[4,64,256]{1,0,2:T(4,128)S(1)}, f32[4,64,256]{1,0,2:T(4,128)}, u32[]{:S(2)}, u32[]{:S(2)}) collective-permute-start(f32[4,64,256]{1,0,2:T(4,128)S(1)} %get-tuple-element.311), channel_id=1, source_target_pairs={{0,1},{1,2},{2,3},{3,4},{4,5},{5,6},{6,7},{7,8},{8,9},{9,10},{10,1... | collective-permute-start | bytes 786440 | tf_op jit(solution)/shard_map/while/body/eval_jaxpr/ppermute | solution.py:16
  895.1 11.1 %collective-permute-start.1 = (f32[4,64,256]{1,0,2:T(4,128)S(1)}, f32[4,64,256]{1,0,2:T(4,128)S(1)}, u32[]{:S(2)}, u32[]{:S(2)}) collective-permute-start(f32[4,64,256]{1,0,2:T(4,128)S(1)} %get-tuple-element.312), channel_id=1, source_target_pairs={{1,0},{2,1},{3,2},{4,3},{5,4},{6,5},{7,6},{8,7},{9,8},{10,9},{11,1... | collective-permute-start | bytes 786440 | tf_op jit(solution)/shard_map/while/body/eval_jaxpr/ppermute | solution.py:17
  897.1 15.4 %collective-permute-start = (f32[4,64,256]{1,0,2:T(4,128)S(1)}, f32[4,64,256]{1,0,2:T(4,128)}, u32[]{:S(2)}, u32[]{:S(2)}) collective-permute-start(f32[4,64,256]{1,0,2:T(4,128)S(1)} %get-tuple-element.311), channel_id=1, source_target_pairs={{0,1},{1,2},{2,3},{3,4},{4,5},{5,6},{6,7},{7,8},{8,9},{9,10},{10,1... | collective-permute-start | bytes 786440 | tf_op jit(solution)/shard_map/while/body/eval_jaxpr/ppermute | solution.py:16
  (64 other events, 133.8 us)
Sparse Core Ops, SparseCore 0:
  933.8 26.5 reduce-scatter.1
where the time goes:
time: 971 us; the launch traced here: 967 us
  blocking collectives  465 us (48%)
  other arithmetic  184 us (19%)
  waiting for transfers between devices  138 us (14%)
  local copies, waits for them, and re-layouts  84.5 us (9%)
  starting transfers between devices  70.2 us (7%)
  between operations  14.7 us (2%)
  matrix products  10.6 us (1%)
    all_gather x1, blocking collectives, shards(): lax.all_gather(owner_row[None, :], 'space', axis=1, tiled=True)  158 us
    all_gather x1, blocking collectives, shards(): piece_traces = lax.all_gather(traces, 'space', axis=1, tiled=True)  157 us
    all_gather x1, blocking collectives, shards(): lax.all_gather(surface[None, :], 'space', axis=1, tiled=True)  150 us
    add x12, other arithmetic, advance(): fresh = 2.0 * current - later + courant_sq * laplace_rim(extended)  122 us
    while x156, local copies, waits for them, and re-layouts  67.3 us
    ppermute x12, waiting for transfers between devices, extended_2(): after = lax.ppermute(leading, axis, down)  61.5 us
    ppermute x12, waiting for transfers between devices, extended_2(): before = lax.ppermute(last, axis, up)  50.6 us
    ppermute x12, starting transfers between devices, extended_2(): before = lax.ppermute(last, axis, up)  45.8 us
  transfers between devices with their start and end apart: 25, of which 25 were waited for; matrix products, arithmetic and copies ran while one was open for 0% of the time, Pallas kernels for 0%

commit v1 on v0

v1 whole, which is shorter than its diff:
```python
import functools

import jax
import jax.numpy as jnp
from jax import lax
from jax.experimental import pallas as pl
from jax.experimental.pallas import tpu as pltpu
from jax.sharding import PartitionSpec as P

WEIGHTS = (-205.0 / 72.0, 8.0 / 5.0, -1.0 / 5.0, 8.0 / 315.0, -1.0 / 560.0)
REACH = 4
LANES = 128
PAD = 8
ROWS = 16
SLOTS = 8
FIELDS = 16
MESH = pl.DeviceIdType.MESH


def kernel(
    ring,
    blocks,
    traces,
    owners,
    cells,
    count,
    current_hbm,
    later_hbm,
    forward_hbm,
    courant_hbm,
    field_hbm,
    total_hbm,
    even,
    odd,
    courant,
    forward,
    gradient,
    listed,
    parted,
    along,
    turned,
    arrived,
    stacked,
    planes,
    from_core_x,
    from_core,
    from_x,
    load_sem,
    forward_sem,
    send_sem,
    recv_sem,
    along_sem,
    across_sem,
    sum_sem,
    out_sem,
):
    shot, space = lax.axis_index("shot"), lax.axis_index("space")
    last = ring * blocks - 1
    spot, block = lax.rem(space, ring), lax.div(space, ring)
    other_core = shot + 1 - 2 * lax.rem(shot, 2)
    other_x = lax.rem(shot + 2, 4)
    length, across, height = courant.shape
    steps, receivers = traces.shape
    own = slice(REACH, REACH + length)
    middle = slice(PAD, PAD + across)
    halves = [slice(0, LANES), slice(LANES, 2 * LANES)]

    loads = []
    for at, (source, target) in enumerate(((current_hbm, even), (later_hbm, odd))):
        for half in range(2):
            loads.append(
                pltpu.make_async_copy(
                    source.at[:, :, halves[half]],
                    target.at[own, half, middle, :],
                    load_sem.at[2 * at + half],
                )
            )
    loads.append(pltpu.make_async_copy(courant_hbm, courant, load_sem.at[4]))
    for load in loads:
        load.start()

    def forward_load(step):
        return pltpu.make_async_copy(
            forward_hbm.at[step], forward.at[step], forward_sem.at[step]
        )

    for field in (even, odd):
        zero = jnp.zeros((length, 2, PAD, LANES), jnp.float32)
        field[own, :, 0:PAD, :] = zero
        field[own, :, PAD + across : 2 * PAD + across, :] = zero

        @pl.when(space == 0)
        def _():
            field[0:REACH] = jnp.zeros((REACH,) + field.shape[1:], jnp.float32)

        @pl.when(space == last)
        def _():
            field[REACH + length :] = jnp.zeros((REACH,) + field.shape[1:], jnp.float32)

    gradient[...] = jnp.zeros_like(gradient)
    if ring * blocks < 64:
        along[...] = jnp.zeros_like(along)
        arrived[...] = jnp.zeros_like(arrived)

    barrier = pltpu.get_barrier_semaphore()

    def greet(**where):
        pl.semaphore_signal(barrier, inc=1, device_id=where, device_id_type=MESH)

    def ring_peer(offset):
        return lax.rem(spot + offset, ring)

    def block_peer(offset):
        return lax.rem(block + offset, blocks)

    @pl.when(space > 0)
    def _():
        greet(space=space - 1)

    @pl.when(space < last)
    def _():
        greet(space=space + 1)

    for offset in range(1, ring):
        greet(space=block * ring + ring_peer(offset))
    for offset in range(1, blocks):
        greet(space=block_peer(offset) * ring + spot)
    greet(shot=other_core)
    greet(shot=other_x)

    for step in range(steps):
        forward_load(step).start()

    row = lax.broadcasted_iota(jnp.int32, (64, receivers), 0)
    owner_of_row = (row & 7) * ring + (row >> 3)
    if ring * blocks < 64:
        real = ((row & 7) < blocks) & ((row >> 3) < ring)
        owner_of_row = jnp.where(real, owner_of_row, -1)
    hot = jnp.where(owners[...] == owner_of_row, 1.0, 0.0).astype(jnp.float32)
    earlier = jnp.where(
        lax.broadcasted_iota(jnp.int32, (receivers, receivers), 0)
        < lax.broadcasted_iota(jnp.int32, (receivers, receivers), 1),
        1.0,
        0.0,
    ).astype(jnp.float32)
    before = jnp.dot(hot, earlier, preferred_element_type=jnp.float32)
    rank = jnp.sum(hot * before, axis=0, keepdims=True).astype(jnp.int32)
    number = space * receivers + lax.broadcasted_iota(jnp.int32, (steps, receivers), 1)
    listed[...] = jnp.zeros_like(listed)
    listed[0:steps, :] = jnp.where(number < count[0], traces[...], 0.0)
    listed[steps : steps + 1, :] = cells[...].astype(jnp.float32)
    tiled = jnp.concatenate([listed[...]] * SLOTS, axis=0)
    slot = lax.broadcasted_iota(jnp.int32, tiled.shape, 0) >> 4
    placed = jnp.where(rank == slot, tiled, 0.0)
    parted[...] = lax.dot_general(
        hot,
        placed,
        (((1,), (1,)), ((), ())),
        precision=lax.Precision.HIGHEST,
        preferred_element_type=jnp.float32,
    ).reshape(parted.shape)

    ends = jnp.where(space == 0, 1, 0) + jnp.where(space == last, 1, 0)
    pl.semaphore_wait(barrier, ring + blocks + 2 - ends)

    def chunk_rows(place):
        chunk = (3 - shot, other_x, other_core, shot)[place]
        return pl.multiple_of(chunk * ROWS, ROWS)

    def halo(field, parity, place, way):
        rows = pl.ds(pl.multiple_of(PAD + chunk_rows(place), 8), ROWS)
        begin = (REACH, length)[way]
        end = (REACH + length, 0)[way]
        return pltpu.make_async_remote_copy(
            src_ref=field.at[begin : begin + REACH, :, rows, :],
            dst_ref=field.at[end : end + REACH, :, rows, :],
            send_sem=send_sem.at[parity, place, way],
            recv_sem=recv_sem.at[parity, place, way],
            device_id={"space": space + (-1, 1)[way]},
            device_id_type=MESH,
        )

    def sends(field, parity, place, wait):
        for way, there in ((0, space > 0), (1, space < last)):

            @pl.when(there)
            def _():
                copy = halo(field, parity, place, way)
                if wait:
                    copy.wait_send()
                else:
                    copy.start()

    def arrivals(field, parity, place):
        for way, there in ((0, space < last), (1, space > 0)):

            @pl.when(there)
            def _():
                halo(field, parity, place, way).wait_recv()

    def along_copy(offset):
        return pltpu.make_async_remote_copy(
            src_ref=parted.at[ring_peer(offset)],
            dst_ref=along.at[spot],
            send_sem=along_sem.at[0, offset],
            recv_sem=along_sem.at[1, offset],
            device_id={"space": block * ring + ring_peer(offset)},
            device_id_type=MESH,
        )

    for offset in range(1, ring):
        along_copy(offset).start()
    along[spot] = parted[spot]

    for load in loads[:2]:
        load.wait()
    for place in range(4):
        sends(even, 0, place, False)

    for offset in range(1, ring):
        along_copy(offset).wait_recv()
    for target in range(blocks):
        turned[target] = along[:, target, :]

    def across_copy(offset):
        return pltpu.make_async_remote_copy(
            src_ref=turned.at[block_peer(offset)],
            dst_ref=arrived.at[block],
            send_sem=across_sem.at[0, offset],
            recv_sem=across_sem.at[1, offset],
            device_id={"space": block_peer(offset) * ring + spot},
            device_id_type=MESH,
        )

    for offset in range(1, blocks):
        across_copy(offset).start()
    arrived[block] = turned[block]
    for load in loads[2:]:
        load.wait()
    for offset in range(1, blocks):
        across_copy(offset).wait_recv()

    rows64 = arrived[...].reshape(64, LANES)
    turned_rows = jnp.concatenate([rows64, jnp.zeros_like(rows64)], axis=0).T
    lane64 = lax.broadcasted_iota(jnp.int32, (64, LANES), 1)
    for at in range(SLOTS):
        moved = pltpu.roll(rows64, (LANES - at * FIELDS) % LANES, 1) if at else rows64
        moved = jnp.where(lane64 < FIELDS, moved, 0.0)
        high = moved.astype(jnp.bfloat16).astype(jnp.float32)
        rest = moved - high
        mid = rest.astype(jnp.bfloat16).astype(jnp.float32)
        low = rest - mid
        parts = high + pltpu.roll(mid, FIELDS, 1) + pltpu.roll(low, 2 * FIELDS, 1)
        begin = (at % 4) * LANES + (at // 4) * 64
        stacked[begin : begin + 64, :] = parts.astype(jnp.bfloat16)
    cell_rows = []
    for at in range(4):
        first = at * FIELDS + steps
        second = (at + 4) * FIELDS + steps
        cell_rows.append(
            turned_rows[first : first + 1, :]
            + pltpu.roll(turned_rows[second : second + 1, :], 64, 1)
        )
    cell_row = jnp.concatenate(cell_rows, axis=1).astype(jnp.int32)
    for at in range(4):
        cell = at * LANES + lax.broadcasted_iota(jnp.int32, (LANES, 4 * LANES), 0)
        table = jnp.where(cell == cell_row, 1.0, 0.0).astype(jnp.bfloat16)
        summed = jnp.dot(table, stacked[...], preferred_element_type=jnp.float32)
        summed = (
            summed
            + pltpu.roll(summed, LANES - FIELDS, 1)
            + pltpu.roll(summed, LANES - 2 * FIELDS, 1)
        )
        planes[at * LANES : (at + 1) * LANES, :] = summed

    lane = lax.broadcasted_iota(jnp.int32, (ROWS, LANES), 1)
    zeros = jnp.zeros((ROWS, LANES), jnp.float32)

    def compute(step, field, fresh_field, place):
        y = chunk_rows(place)
        rows = pl.ds(pl.multiple_of(PAD + y, 8), ROWS)
        flat = pl.ds(y, ROWS)
        for x in range(length):
            at = x + REACH
            centers = [field[at, half, rows, :] for half in range(2)]
            sums = [3.0 * WEIGHTS[0] * centers[half] for half in range(2)]
            for j in range(1, REACH + 1):
                up = [pltpu.roll(center, j, 1) for center in centers]
                down = [pltpu.roll(center, LANES - j, 1) for center in centers]
                z_taps = [
                    jnp.where(lane < j, zeros, up[0]) + jnp.where(lane < LANES - j, down[0], down[1]),
                    jnp.where(lane < j, up[0], up[1]) + jnp.where(lane < LANES - j, down[1], zeros),
                ]
                for half in range(2):
                    taps = field[at + j, half, rows, :] + field[at - j, half, rows, :]
                    taps = taps + field[at, half, pl.ds(PAD + y + j, ROWS), :]
                    taps = taps + field[at, half, pl.ds(PAD + y - j, ROWS), :]
                    sums[half] = sums[half] + WEIGHTS[j] * (taps + z_taps[half])
            for half in range(2):
                fresh = 2.0 * centers[half] - fresh_field[at, half, rows, :]
                fresh = fresh + courant[x, flat, halves[half]] * sums[half]
                if half == 0:
                    cell_at = pl.ds(pl.multiple_of(x * across + y, ROWS), ROWS)
                    source = pltpu.roll(planes[cell_at, :], lax.rem(LANES + 2 - step, LANES), 1)
                    fresh = fresh + jnp.where(lane == 2, source, 0.0)
                fresh_field[at, half, rows, :] = fresh
                accel = forward[step, x, flat, halves[half]].astype(jnp.float32)
                gradient[x, flat, halves[half]] += fresh * accel

    def reduce_copy(at, rows, target, peer):
        return pltpu.make_async_remote_copy(
            src_ref=gradient.at[:, rows, :],
            dst_ref=target,
            send_sem=sum_sem.at[0, at],
            recv_sem=sum_sem.at[1, at],
            device_id={"shot": peer},
            device_id_type=MESH,
        )

    def to_owner(place):
        target = (from_core_x, from_x, from_core)[place]
        peer = (other_core, other_x, other_core)[place]
        return reduce_copy(place, pl.ds(chunk_rows(place), ROWS), target, peer)

    def result_copies(place):
        y = chunk_rows(place)
        rows = pl.ds(pl.multiple_of(PAD + y, 8), ROWS)
        return [
            pltpu.make_async_copy(
                even.at[own, half, rows, :],
                field_hbm.at[:, pl.ds(y, ROWS), halves[half]],
                out_sem.at[2 * place + half],
            )
            for half in range(2)
        ]

    def two_steps(pair, carry):
        first, second = 2 * pair, 2 * pair + 1
        forward_load(first).wait()
        for place in range(4):
            arrivals(even, 0, place)

            @pl.when(pair > 0)
            def _():
                sends(odd, 1, place, True)

            compute(first, even, odd, place)
            sends(odd, 1, place, False)
        forward_load(second).wait()
        for place in range(4):
            arrivals(odd, 1, place)
            sends(even, 0, place, True)
            compute(second, odd, even, place)

            @pl.when(pair < steps // 2 - 1)
            def _():
                sends(even, 0, place, False)

            @pl.when(pair == steps // 2 - 1)
            def _():
                for copy in result_copies(place):
                    copy.start()
                if place == 1:
                    to_owner(0).wait_recv()
                    rows = pl.ds(chunk_rows(1), ROWS)
                    gradient[:, rows, :] += from_core_x[...]
                if place < 3:
                    to_owner(place).start()

        return carry

    lax.fori_loop(0, steps // 2, two_steps, 0)

    to_owner(2).wait_recv()
    rows = pl.ds(chunk_rows(3), ROWS)
    partial = gradient[:, rows, :] + from_core[...]
    to_owner(1).wait_recv()
    from_core[...] = partial + from_x[...]
    result = pltpu.make_async_copy(from_core, total_hbm, load_sem.at[0])
    result.start()
    for place in range(4):
        sends(odd, 1, place, True)
        for copy in result_copies(place):
            copy.wait()
    for place in range(3):
        to_owner(place).wait_send()
    for offset in range(1, ring):
        along_copy(offset).wait_send()
    for offset in range(1, blocks):
        across_copy(offset).wait_send()
    result.wait()


def shards(
    ring,
    blocks,
    residual_traces,
    owners,
    surface_cells,
    trace_counts,
    start_current,
    start_later,
    forward_accel,
    courant_sq,
):
    length, across, height = courant_sq.shape
    steps = residual_traces.shape[1]
    receivers = residual_traces.shape[2]
    field = pltpu.VMEM((length + 2 * REACH, 2, across + 2 * PAD, LANES), jnp.float32)
    piece = pltpu.VMEM((length, ROWS, height), jnp.float32)
    vmem = pl.BlockSpec(memory_space=pltpu.VMEM)
    anywhere = pl.BlockSpec(memory_space=pl.ANY)
    adjoint, total = pl.pallas_call(
        functools.partial(kernel, ring, blocks),
        out_shape=(
            jax.ShapeDtypeStruct((length, across, height), jnp.float32),
            jax.ShapeDtypeStruct((length, ROWS, height), jnp.float32),
        ),
        in_specs=[vmem, vmem, vmem, pl.BlockSpec(memory_space=pltpu.SMEM)] + [anywhere] * 4,
        out_specs=(anywhere, anywhere),
        scratch_shapes=[
            field,
            field,
            pltpu.VMEM((length, across, height), jnp.float32),
            pltpu.VMEM((steps, length, across, height), jnp.bfloat16),
            pltpu.VMEM((length, across, height), jnp.float32),
            pltpu.VMEM((FIELDS, receivers), jnp.float32),
            pltpu.VMEM((8, 8, LANES), jnp.float32),
            pltpu.VMEM((8, 8, LANES), jnp.float32),
            pltpu.VMEM((8, 8, LANES), jnp.float32),
            pltpu.VMEM((8, 8, LANES), jnp.float32),
            pltpu.VMEM((4 * LANES, LANES), jnp.bfloat16),
            pltpu.VMEM((length * across, LANES), jnp.float32),
            piece,
            piece,
            piece,
            pltpu.SemaphoreType.DMA((5,)),
            pltpu.SemaphoreType.DMA((steps,)),
            pltpu.SemaphoreType.DMA((2, 4, 2)),
            pltpu.SemaphoreType.DMA((2, 4, 2)),
            pltpu.SemaphoreType.DMA((2, 8)),
            pltpu.SemaphoreType.DMA((2, 8)),
            pltpu.SemaphoreType.DMA((2, 3)),
            pltpu.SemaphoreType.DMA((8,)),
        ],
        compiler_params=pltpu.CompilerParams(
            collective_id=0, has_side_effects=True, vmem_limit_bytes=60 * 2**20
        ),
    )(
        residual_traces[0],
        owners[0, :, 0][None, :],
        surface_cells,
        trace_counts,
        start_current[0],
        start_later[0],
        forward_accel[0],
        courant_sq,
    )
    return (adjoint[None], total)


def solution(mesh):
    placed = (
        P("shot", None, "space"),
        P("shot", "space", None),
        P("shot", "space"),
        P("shot"),
        P("shot", "space", None, None),
        P("shot", "space", None, None),
        P("shot", None, "space", None, None),
        P("space", None, None),
    )
    n_space = mesh.shape["space"]
    ring = 8 if n_space == 64 else 2
    return jax.shard_map(
        functools.partial(shards, ring, n_space // ring),
        mesh=mesh,
        in_specs=placed,
        out_specs=(P("shot", "space", None, None), P("space", "shot", None)),
        check_vma=False,
    )
```

time: 971 us -> 103 us (0.11)
  blocking collectives: 465 us -> 0 us
  other arithmetic: 184 us -> 0 us
  waiting for transfers between devices: 138 us -> 0 us
  Pallas kernels: 0 us -> 97.1 us
  local copies, waits for them, and re-layouts: 84.5 us -> 4.75 us
  starting transfers between devices: 70.2 us -> 0 us
  between operations: 14.7 us -> 1.29 us
  matrix products: 10.6 us -> 0 us
    all_gather x3 -> x0, blocking collectives: 465 us -> none  [the longest x1 158 us: shards(): lax.all_gather(owner_row[None, :], 'space', axis=1, tiled=True)]
    add x24 -> x0, other arithmetic: 140 us -> none  [the longest x12 122 us: advance(): fresh = 2.0 * current - later + courant_sq * laplace_rim(extended)]
    ppermute x24 -> x0, waiting for transfers between devices: 112 us -> none  [the longest x12 61.5 us: extended_2(): after = lax.ppermute(leading, axis, down)]
    pallas_call x0 -> x1, Pallas kernels: none -> 97.1 us  [shards(): pl.pallas_call(functools.partial(kernel, ring, blocks), out_shape=(jax.Sh...]
    while x158 -> x0, local copies, waits for them, and re-layouts: 70.8 us -> none
    ppermute x24 -> x0, starting transfers between devices: 70.1 us -> none  [the longest x12 45.8 us: extended_2(): before = lax.ppermute(last, axis, up)]
    concatenate x12 -> x0, other arithmetic: 28.2 us -> none  [extended_2(): shard = jnp.concatenate([before, shard, after], axis=dim)]
    reduce_scatter x1 -> x0, waiting for transfers between devices: 25.5 us -> none  [shards(): lax.psum_scatter(gradient, 'shot', scatter_dimension=1, tiled=True)]
  transfers between devices with their start and end apart: 25 -> 0, of which waited for: 25 -> 0; matrix products, arithmetic and copies ran while one was open for 0% -> 0% of each run, Pallas kernels for 0% -> 0%
where the time goes in v1:
time: 103 us
  Pallas kernels  97.1 us (94%)
  local copies, waits for them, and re-layouts  4.75 us (5%)
  between operations  1.29 us (1%)
    pallas_call x1, Pallas kernels, shards(): pl.pallas_call(functools.partial(kernel, ring, blocks), out_shape=(jax.Sh...  97.1 us
    unnamed x3, local copies, waits for them, and re-layouts  4.75 us

profile of v1, /device:TPU:2, one launch (start us, length us, event | category | flops | bytes accessed | tf_op | source)
XLA Modules:
  0.0 103.1 jit_solution(5997350828178713271)
XLA Ops:
  1.3 1.3 %copy.12 = f32[1,12,256]{2,1,0:T(8,128)} copy(f32[1,12,256]{2,0,1:T(1,128)} %param.8) | data formatting | bytes 24576
  2.6 97.1 %shard_map.95 = (f32[8,64,256]{2,1,0:T(8,128)}, f32[8,16,256]{2,1,0:T(8,128)}) custom-call(f32[12,256]{1,0:T(8,128)} %bitcast.12, s32[1,256]{1,0:T(1,128)} %bitcast.13, s32[1,256]{1,0:T(1,128)} %cells.1, s32[1]{0:T(128)S(6)} %copy.15.count, f32[8,64,256]{2,1,0:T(8,128)} %bitcast.9, f32[8,64,256]{2,1,0:T(8,128)} %bitcast.10, ...), custom_call_target="tpu_custom_call" | custom-call | tf_op jit(solution)/shard_map/pallas_call | solution.py:413
  99.7 1.9 %copy.16 = f32[1,8,64,256]{3,2,1,0:T(8,128)} copy(f32[1,8,64,256]{3,2,1,0:T(8,128)} %bitcast.11) | data formatting | bytes 1048576
  101.5 1.6 %copy.17 = f32[8,16,256]{2,1,0:T(8,128)} copy(f32[8,16,256]{2,1,0:T(8,128)} %get-tuple-element.9) | data formatting | bytes 262144
